TPU v7x, 512 devices: a whole 4x8x8 slice. The times are simulated.
512 devices in a mesh: seq: 64 (over z, x, core), head: 8 (over y).
Axes of the slice: x: 4, y: 8, z: 8, core: 2. Of those that a mesh axis runs over, the one named last changes fastest.
Arguments:
- queries: bfloat16 [32768, 3072], P('seq', 'head'), may hold values from -6 to 6
- key_vectors: bfloat16 [32768, 3072], P('seq', 'head'), may hold values from -6 to 6
- value_vectors: bfloat16 [32768, 3072], P('seq', 'head'), may hold values from -6 to 6
- doc_lengths: int32 [16], replicated, may hold values from 1 to 20480, 32768 in all
- norm_gain: float32 [3072], P('head'), may hold values from 0.1 to 1.9
- out_weight: bfloat16 [3072, 4096], P('head'), may hold values from -0.15625 to 0.15625
Outputs:
- layer_out: bfloat16 [32768, 4096], P('seq', 'head')
Inputs may be any that keep to these rules, and one draw needn't show every extreme that they name: doc_lengths sum to 32768; the longest document has exactly 20480 tokens.
All inputs are finite; a program needn't handle non-finite values.
Results may differ from a plain program's by a relative error of at most 0.014.
Values may be sent and summed in bfloat16 or wider, within the bound.
A program may use at most 64 MiB of HBM per device.

v0:
```python
import jax
import jax.numpy as jnp
from jax import lax
from jax.sharding import PartitionSpec as P

DH = 128


def attend_block(query_h, key_h, value_h, segment):
    row_count = query_h.shape[0]
    row_ids = jnp.arange(row_count, dtype=jnp.int32)
    allowed = (row_ids[None, :] <= row_ids[:, None]) & (segment[None, :] == segment[:, None])
    scores = jnp.einsum("thd,shd->hts", query_h, key_h, preferred_element_type=jnp.float32)
    scores = jnp.where(allowed[None], scores, 0.0).astype(jnp.bfloat16)
    within = jnp.einsum("hts,shd->thd", scores, value_h, preferred_element_type=jnp.float32)
    last_rows = segment == segment[-1]
    key_last = jnp.where(last_rows[:, None, None], key_h, jnp.zeros_like(key_h))
    block_state = jnp.einsum("thd,the->hde", key_last, value_h, preferred_element_type=jnp.float32)
    return (within, block_state)


def body(queries, key_vectors, value_vectors, doc_lengths, norm_gain, out_weight):
    row_count = queries.shape[0]
    head_count = queries.shape[1] // DH
    group_width = head_count * DH
    my_block = lax.axis_index("seq")
    offset = my_block * row_count
    doc_bounds = jnp.cumsum(doc_lengths)
    positions = offset + jnp.arange(row_count, dtype=jnp.int32)
    before = doc_bounds[None, :] <= positions[:, None]
    segment = jnp.sum(before.astype(jnp.int32), axis=1)
    starts = jnp.sum(jnp.where(before, doc_lengths[None, :], 0), axis=1)
    query_h = queries.reshape(row_count, head_count, DH)
    key_h = key_vectors.reshape(row_count, head_count, DH)
    value_h = value_vectors.reshape(row_count, head_count, DH)
    within, block_state = attend_block(query_h, key_h, value_h, segment)
    first_block = starts[0] // row_count
    shards = lax.all_gather(block_state[None], "seq", axis=0, tiled=True)
    shard_ids = jnp.arange(shards.shape[0], dtype=jnp.int32)
    weights = ((shard_ids >= first_block) & (shard_ids < my_block)).astype(jnp.float32)
    carried = jnp.sum(weights[:, None, None, None] * shards, axis=0)
    carried = carried.astype(jnp.bfloat16)
    cross_rows = (segment == segment[0]) & (starts[0] < offset)
    query_cross = jnp.where(cross_rows[:, None, None], query_h, jnp.zeros_like(query_h))
    carried_term = jnp.einsum(
        "thd,hde->the", query_cross, carried, preferred_element_type=jnp.float32
    )
    mixture = within + carried_term
    square_mean = jnp.mean(mixture * mixture, axis=-1, keepdims=True)
    gain_heads = norm_gain.reshape(head_count, DH)
    normed = (mixture * lax.rsqrt(square_mean + 1e-06) * gain_heads).astype(jnp.bfloat16)
    normed = normed.reshape(row_count, group_width)
    partial_sum = jnp.dot(normed, out_weight, preferred_element_type=jnp.float32)
    layer_out = lax.psum_scatter(
        partial_sum.astype(jnp.bfloat16), "head", scatter_dimension=1, tiled=True
    )
    return layer_out


def solution(mesh):
    return jax.shard_map(
        body,
        mesh=mesh,
        in_specs=(
            P("seq", "head"),
            P("seq", "head"),
            P("seq", "head"),
            P(),
            P("head"),
            P("head", None),
        ),
        out_specs=P("seq", "head"),
        check_vma=False,
    )
```

profile of v0, /device:TPU:1, one launch (start us, length us, event | category | flops | bytes accessed | tf_op | source)
XLA Modules:
  0.0 195.1 jit_solution(6924169101903005490)
XLA Ops:
  6.5 0.0 copy-start
  6.5 0.0 all-gather.3.cloned.1.call-start
  6.5 0.9 copy.28
  7.5 0.1 reduce
  7.6 0.7 fusion.13
  8.3 0.6 slice.10
  9.6 0.7 fusion.17
  10.2 1.2 copy.30
  11.4 0.0 copy-start.1
  11.4 2.1 %copy.33 = bf16[512,384]{0,1:T(8,128)(2,1)} copy(bf16[512,384]{1,0:T(8,128)(2,1)} %param.8) | data formatting | bytes 786432 | tf_op args[2]
  13.5 1.3 broadcast_compare_fusion
  14.7 2.0 %fusion.5 = f32[3,128,128]{2,1,0:T(8,128)} fusion(bf16[512,3,128]{0,2,1:T(8,128)(2,1)} %bitcast.29, bf16[512,3,128]{0,2,1:T(8,128)(2,1)S(1)} %bitcast.27, pred[512]{0:T(512)(128)(4,1)S(1)} %get-tuple-element.7), kind=kOutput, calls=%fused_computation.12 | convolution fusion | flops 50528256 | bytes 983552 | tf_op jit(solution)/shard_map/thd,the->hde/dot_general | solution.py:18
  16.7 0.0 all-gather.3.cloned.1.call-update
  16.7 0.0 reduce-scatter.2.cloned.1.call-start
  19.5 0.0 copy-done.1
  19.5 1.2 copy.29
  20.7 0.9 fusion.3
  21.6 96.7 %all-gather.3.cloned.1.call-done = f32[192,128,128]{2,1,0:T(8,128)} async-done(((f32[3,128,128]{2,1,0:T(8,128)}), f32[192,128,128]{2,1,0:T(8,128)}) %all-gather.3.cloned.1.call-update) | async-done | bytes 12582928 | tf_op jit(solution)/shard_map/all_gather | solution.py:38
  118.3 5.9 %multiply_reduce_fusion = bf16[3,128,128]{2,1,0:T(8,128)(2,1)S(1)} fusion(f32[64,3,128,128]{3,2,1,0:T(8,128)} %bitcast.23, f32[64]{0:T(128)S(1)} %and_convert_fusion), kind=kLoop, calls=%fused_computation | loop fusion | flops 6242304 | bytes 12681472 | tf_op jit(solution)/shard_map/reduce_sum | solution.py:41
  124.2 0.0 copy-start.2
  124.2 1.2 convolution_bitcast_fusion
  125.4 3.4 %multiply_reduce_fusion.1 = (f32[512,3]{0,1:T(4,128)S(1)}, f32[512,3,128]{0,2,1:T(8,128)}) fusion(f32[512,3,128]{0,2,1:T(8,128)} %convolution_bitcast_fusion, bf16[512,3,128]{0,2,1:T(8,128)(2,1)} %bitcast.30, bf16[512,3,128]{0,2,1:T(8,128)(2,1)S(1)} %bitcast.25, bf16[512,3,128]{0,2,1:T(8,128)(2,1)} %bitcast.28, pred[512,512]{1,0:T(8,128)(4,1)} %fusion.3), kind=kOutput, calls=%fused_computation.10 | convolution fusion | flops 404814336 | bytes 3020800 | tf_op jit(solution)/shard_map/hts,shd->thd/dot_general | solution.py:15
  128.8 0.0 copy-done.2
  128.8 1.3 multiply_convert_fusion
  130.1 0.0 copy-done
  130.1 4.3 %convolution_convert_fusion = bf16[512,4096]{1,0:T(8,128)(2,1)} fusion(bf16[512,384]{0,1:T(8,128)(2,1)S(1)} %bitcast.26, bf16[384,4096]{1,0:T(8,128)(2,1)S(1)} %copy-done), kind=kOutput, calls=%fused_computation.1 | convolution fusion | flops 1612709888 | bytes 7733248 | tf_op jit(solution)/shard_map/dot_general | solution.py:53
  134.4 0.0 reduce-scatter.2.cloned.1.call-update
  134.4 53.8 %reduce-scatter.2.cloned.1.call-done = bf16[512,512]{1,0:T(8,128)(2,1)} async-done(((bf16[512,4096]{1,0:T(8,128)(2,1)}), bf16[512,512]{1,0:T(8,128)(2,1)}) %reduce-scatter.2.cloned.1.call-update) | async-done | bytes 524304 | tf_op jit(solution)/shard_map/reduce_scatter | solution.py:54
  (4 shorter events, 0.1 us)
Async XLA Ops:
  6.5 123.5 %copy-start = (bf16[384,4096]{1,0:T(8,128)(2,1)S(1)}, bf16[384,4096]{1,0:T(8,128)(2,1)}, u32[]{:S(2)}) copy-start(bf16[384,4096]{1,0:T(8,128)(2,1)} %param.11) | copy-start | bytes 9437188
  6.5 111.7 %all-gather.3.cloned.1.call-start = ((), (), s32[]{:S(2)}) async-start(), calls=%async_computation.2 | async-start | bytes 12779520 | tf_op jit(solution)/shard_map/all_gather | solution.py:38
  11.4 8.0 %copy-start.1 = (bf16[512,384]{0,1:T(8,128)(2,1)}, bf16[512,384]{0,1:T(8,128)(2,1)S(1)}, u32[]{:S(2)}) copy-start(bf16[512,384]{0,1:T(8,128)(2,1)S(1)} %copy.30) | copy-start | bytes 1179652
  16.7 171.5 %reduce-scatter.2.cloned.1.call-start = ((), (), s32[]{:S(2)}) async-start(), calls=%async_computation.1 | async-start | bytes 4718592 | tf_op jit(solution)/shard_map/reduce_scatter | solution.py:54
  124.2 4.6 %copy-start.2 = (f32[384]{0:T(512)S(1)}, f32[384]{0:T(512)}, u32[]{:S(2)}) copy-start(f32[384]{0:T(512)} %param.10) | copy-start | bytes 4612
Sparse Core Ops, SparseCore 0:
  16.8 101.3 all-gather.2
  134.5 53.6 reduce-scatter.1
where the time goes:
time: 195 us
  waiting for transfers between devices  151 us (77%)
  between operations  16.9 us (9%)
  matrix products  10.9 us (6%)
  other arithmetic  10.2 us (5%)
  local copies, waits for them, and re-layouts  6.53 us (3%)
    all_gather x1, waiting for transfers between devices, body(): shards = lax.all_gather(block_state[None], 'seq', axis=0, tiled=True)  96.7 us
    reduce_scatter x1, waiting for transfers between devices, body(): lax.psum_scatter(partial_sum.astype(jnp.bfloat16), 'head', scatter_dimens...  53.8 us
    reduce_sum x1, other arithmetic, body(): carried = jnp.sum(weights[:, None, None, None] * shards, axis=0)  5.87 us
    unnamed x9, local copies, waits for them, and re-layouts  4.41 us
    dot_general x1, matrix products, body(): jnp.dot(normed, out_weight, preferred_element_type=jnp.float32)  4.31 us
  transfers between devices with their start and end apart: 2, of which 2 were waited for; matrix products, arithmetic and copies ran while one was open for 1% of the time, Pallas kernels for 0%

commit v1 on v0

v1 whole, which is shorter than its diff:
```python
import functools

import jax
import jax.numpy as jnp
from jax import lax
from jax.experimental import pallas as pl
from jax.experimental.pallas import tpu as pltpu
from jax.sharding import PartitionSpec as P

DH = 128
ROW = 8
MESH = pl.DeviceIdType.MESH
F32 = jnp.float32
BF16 = jnp.bfloat16


def dot(a, b, dims=((1,), (0,))):
    return lax.dot_general(a, b, (dims, ((), ())), preferred_element_type=F32)


def layer_kernel(
    nz, row, ny,
    q_any, k_any, v_any, lens, gain, w_any, out_any,
    q_ref, k_ref, v_ref, s_loc, s_in, r_in, crow, c_out, c_in, lo_ref, within, norm_all, wcol, acc, out_v,
    load_sem, p1s, p1r, p2s, p2r, p3s, p3r, wys, wyr, wxs, wxr, wzs, wzr, wcs, wcr, ys, yr,
):
    tok, width = q_ref.shape
    heads = width // DH
    cols = out_v.shape[1]
    nx = row // 2
    yh, zh = ny // 2, nz // 2
    sl = width // row
    wr = width // nz
    xc = cols // nx
    seq, y = lax.axis_index("seq"), lax.axis_index("head")
    z, r = seq // row, seq % row
    x, c = r // 2, r % 2
    sends = []

    def remote(src, dst, ssem, rsem, target):
        return pltpu.make_async_remote_copy(
            src_ref=src, dst_ref=dst, send_sem=ssem, recv_sem=rsem,
            device_id=target, device_id_type=MESH)

    def send(*args):
        copy = remote(*args)
        copy.start()
        sends.append(copy)

    def row_dev(i):
        return (z * row + i, y)

    def z_dev(i):
        return (i * row + r, y)

    def y_dev(i):
        return (seq, i)

    barrier = pltpu.get_barrier_semaphore()
    peers = [row_dev((r + k) % row) for k in range(1, row)]
    peers += [z_dev((z + k) % nz) for k in range(1, nz)]
    peers += [y_dev((y + k) % ny) for k in range(1, ny)]
    for peer in peers:
        pl.semaphore_signal(barrier, inc=1, device_id=peer, device_id_type=MESH)

    loads = [
        pltpu.make_async_copy(k_any, k_ref, load_sem.at[0]),
        pltpu.make_async_copy(v_any, v_ref, load_sem.at[1]),
        pltpu.make_async_copy(q_any, q_ref, load_sem.at[2]),
        pltpu.make_async_copy(
            w_any.at[:, pl.ds(pl.multiple_of(y * cols, 128), cols)], wcol.at[0], load_sem.at[3]),
    ]
    for load in loads:
        load.start()

    bounds, total = [], jnp.int32(0)
    for d in range(lens.shape[0]):
        total = total + lens[d]
        bounds.append(total)

    def start_of(position):
        found = jnp.int32(0)
        for bound in bounds:
            found = jnp.where(bound <= position, bound, found)
        return found

    def flag(condition):
        return jnp.where(condition, jnp.float32(1), jnp.float32(0))

    offset = seq * tok
    lo_last = start_of(offset + (tok - 1)) - offset
    first = z * row
    row_start = [start_of((first + i) * tok) for i in range(row)]
    next_start = start_of((first + row) * tok)
    w_row_sum = [flag((first + j + 1) * tok > next_start) for j in range(row)]
    w_past = [flag(row_start[i] < first * tok) for i in range(row)]
    w_rows = [flag(((i + 1) * row * tok > row_start[0]) & (i < z)) for i in range(nz)]

    rows = lax.broadcasted_iota(jnp.int32, (tok, DH), 0)
    keep = flag(rows >= lo_last)
    loads[0].wait()
    loads[1].wait()
    for h in range(heads):
        hs = slice(h * DH, (h + 1) * DH)
        key = (k_ref[:, hs].astype(F32) * keep).astype(BF16)
        s_loc[hs, :] = dot(key, v_ref[:, hs], ((0,), (0,))).astype(BF16)

    pl.semaphore_wait(barrier, len(peers))

    def part(i):
        return pl.ds(pl.multiple_of(i * sl, 16), sl)

    for k in range(1, row):
        i = (r + k) % row
        send(s_loc.at[part(i)], s_in.at[r], p1s.at[k], p1r.at[k], row_dev(i))

    first_rel = 1 + (yh - 1) * c
    z_rows = pl.ds(pl.multiple_of(z * wr, 16), wr)
    x_cols = pl.ds(pl.multiple_of(x * xc, 128), xc)
    for i in range(yh):
        rel = first_rel + i
        plane = (y + ny - rel) % ny
        send(
            w_any.at[z_rows, pl.ds(pl.multiple_of(plane * cols + x * xc, 128), xc)],
            wcol.at[rel, z_rows, x_cols], wys.at[i], wyr.at[i], y_dev(plane))

    s_in[r] = s_loc[part(r), :]
    lo = jnp.zeros((tok, DH), jnp.int32) - offset
    for bound in bounds:
        lo = jnp.where(rows >= bound - offset, bound - offset, lo)
    lo_ref[...] = lo
    loads[2].wait()

    tb = tok // 2

    def attend(h):
        hs = slice(h * DH, (h + 1) * DH)
        for b in range(2):
            upto = (b + 1) * tb
            ts = slice(b * tb, upto)
            scores = dot(q_ref[ts, hs], k_ref[:upto, hs], ((1,), (1,)))
            t_ids = lax.broadcasted_iota(jnp.int32, (tb, upto), 0) + b * tb
            s_ids = lax.broadcasted_iota(jnp.int32, (tb, upto), 1)
            low = jnp.broadcast_to(lo_ref[ts, 0:1], (tb, upto))
            allowed = (s_ids <= t_ids) & (s_ids >= low)
            scores = jnp.where(allowed, scores, 0.0).astype(BF16)
            within[h, ts, :] = dot(scores, v_ref[:upto, hs])

    attend(0)

    for k in range(1, row):
        j = (r + row - k) % row
        remote(s_loc.at[part(j)], s_in.at[j], p1s.at[k], p1r.at[k], row_dev(j)).wait_recv()

    state = [s_in[j].astype(F32) for j in range(row)]
    row_sum = functools.reduce(jnp.add, [w_row_sum[j] * state[j] for j in range(row)])
    r_in[z] = row_sum.astype(BF16)
    for k in range(1, nz):
        send(r_in.at[z], r_in.at[z], p2s.at[k], p2r.at[k], z_dev((z + k) % nz))

    rels = pl.ds(first_rel, yh)
    for i in range(yh):
        rel = first_rel + i
        remote(
            w_any.at[z_rows, pl.ds(0, xc)], wcol.at[rel, z_rows, x_cols],
            wys.at[i], wyr.at[i], y_dev((y + rel) % ny)).wait_recv()
    for k in range(1, nx):
        block = wcol.at[rels, z_rows, x_cols]
        send(block, block, wxs.at[k], wxr.at[k], row_dev((x + k) % nx * 2 + c))

    for i in range(row):
        total = jnp.zeros((sl, DH), F32)
        for j in range(i):
            total = total + flag((first + j + 1) * tok > row_start[i]) * state[j]
        crow[i] = total
    attend(1)

    for k in range(1, nz):
        i = (z + nz - k) % nz
        remote(r_in.at[i], r_in.at[i], p2s.at[k], p2r.at[k], z_dev(i)).wait_recv()

    past = functools.reduce(jnp.add, [w_rows[i] * r_in[i].astype(F32) for i in range(nz)])
    for i in range(row):
        c_out[i] = (crow[i] + w_past[i] * past).astype(BF16)
    for k in range(1, row):
        i = (r + k) % row
        send(c_out.at[i], c_in.at[part(r)], p3s.at[k], p3r.at[k], row_dev(i))
    c_in[part(r), :] = c_out[r]

    attend(2)

    for k in range(1, nx):
        i = (x + nx - k) % nx
        block = wcol.at[rels, z_rows, pl.ds(pl.multiple_of(i * xc, 128), xc)]
        remote(block, block, wxs.at[k], wxr.at[k], row_dev(i * 2 + c)).wait_recv()

    def z_block(i, first, count):
        return wcol.at[pl.ds(first, count), pl.ds(pl.multiple_of(i * wr, 16), wr), :]

    def z_copy(way, d, starting):
        step = 1 if way == 0 else nz - 1
        away = d if starting else d + 1
        owner = (z + away * (nz - step)) % nz
        if d < zh - 1:
            block = z_block(owner, first_rel, yh)
        elif way == 0:
            block = z_block(owner, first_rel, yh // 2)
        else:
            block = z_block(owner, first_rel + yh // 2, yh - yh // 2)
        return block, block, wzs.at[way, d], wzr.at[way, d], z_dev((z + step) % nz)

    own_rels, twin_rels = 1 + yh * c, 1 + yh * (1 - c)
    twin = row_dev(x * 2 + (1 - c))

    def to_twin(i, n):
        block = z_block(i, own_rels, yh - 1)
        send(block, block, wcs.at[n], wcr.at[n], twin)

    def z_step(d):
        if d > 0:
            for way in range(2):
                remote(*z_copy(way, d - 1, False)).wait_recv()
        if d < zh:
            for way in range(2):
                send(*z_copy(way, d, True))
        if d == 0 or d == zh:
            to_twin((z + d) % nz, d)
        else:
            to_twin((z + d) % nz, d)
            to_twin((z + nz - d) % nz, nz - d)

    def twin_wait():
        for n in range(nz):
            block = z_block((z + n) % nz, twin_rels, yh - 1)
            remote(block, block, wcs.at[n], wcr.at[n], twin).wait_recv()

    z_step(0)

    for k in range(1, row):
        j = (r + row - k) % row
        remote(c_out.at[j], c_in.at[part(j)], p3s.at[k], p3r.at[k], row_dev(j)).wait_recv()

    def y_copy(way, d, h, starting):
        slot = (ny - d) % ny if way == 0 else d
        later = ny - d - 1 if way == 0 else d + 1
        ts = pl.ds(0, tok)
        if d == yh - 1:
            ts = pl.ds(way * tb, tb)
        src, dst = norm_all.at[slot, h, ts], norm_all.at[later, h, ts]
        to = (y + 1) % ny if way == 0 else (y + ny - 1) % ny
        return src, dst, ys.at[way, d, h], yr.at[way, d, h], y_dev(to)

    def y_send(d, h):
        for way in range(2):
            send(*y_copy(way, d, h, True))

    def y_wait(d, h, ways=(0, 1)):
        for way in ways:
            remote(*y_copy(way, d - 1, h, False)).wait_recv()

    for h in range(heads):
        hs = slice(h * DH, (h + 1) * DH)
        carried = c_in[hs, :]
        scale = gain[:, hs]
        for b in range(2):
            ts = slice(b * tb, (b + 1) * tb)
            term = dot(q_ref[ts, hs], carried)
            mixture = within[h, ts, :] + jnp.where(lo_ref[ts, :] < 0, term, 0.0)
            square_mean = jnp.mean(mixture * mixture, axis=-1, keepdims=True)
            norm_all[0, h, ts, :] = (mixture * lax.rsqrt(square_mean + 1e-06) * scale).astype(BF16)
        y_send(0, h)

    def project(rel, start=False):
        for b in range(2):
            ts = slice(b * tb, (b + 1) * tb)
            left = jnp.concatenate([norm_all[rel, h, ts, :] for h in range(heads)], axis=1)
            term = dot(left, wcol[rel])
            acc[ts, :] = term if start else acc[ts, :] + term

    def y_step(d, h):
        y_wait(d, h)
        y_send(d, h)

    loads[3].wait()
    project(0, True)
    z_left = list(range(1, zh + 1))
    n = 0
    for d in range(1, yh):
        if d == yh - 1:
            while z_left:
                z_step(z_left.pop(0))
            twin_wait()
            for e in range(1, d):
                project(e)
                project(ny - e)
        for h in range(heads):
            y_step(d, h)
            n += 1
            if n in (1, 3, 5, 6) and z_left:
                z_step(z_left.pop(0))
    project(yh - 1)
    project(yh + 1)
    for h in range(heads):
        hs = slice(h * DH, (h + 1) * DH)
        for way in range(2):
            ts = slice(way * tb, (way + 1) * tb)
            y_wait(yh, h, (way,))
            total = acc[ts, :] + dot(norm_all[yh, h, ts, :], wcol[yh, hs, :])
            if h < heads - 1:
                acc[ts, :] = total
            else:
                out_v[ts, :] = total.astype(BF16)
                load_sem_way = load_sem.at[way]
                pltpu.make_async_copy(out_v.at[ts], out_any.at[ts], load_sem_way).start()
    for copy in sends:
        copy.wait_send()
    for way in range(2):
        ts = slice(way * tb, (way + 1) * tb)
        pltpu.make_async_copy(out_v.at[ts], out_any.at[ts], load_sem.at[way]).wait()


def body(nz, row, ny, queries, key_vectors, value_vectors, doc_lengths, norm_gain, out_weight):
    tok, width = queries.shape
    heads = width // DH
    cols = out_weight.shape[1] // ny
    yh, zh = ny // 2, nz // 2
    sl = width // row
    dma = pltpu.SemaphoreType.DMA
    any_spec = pl.BlockSpec(memory_space=pl.ANY)
    return pl.pallas_call(
        functools.partial(layer_kernel, nz, row, ny),
        name="layer",
        out_shape=jax.ShapeDtypeStruct((tok, cols), BF16),
        in_specs=[
            any_spec, any_spec, any_spec,
            pl.BlockSpec(memory_space=pltpu.SMEM),
            pl.BlockSpec(memory_space=pltpu.VMEM),
            any_spec,
        ],
        out_specs=any_spec,
        scratch_shapes=[
            pltpu.VMEM((tok, width), BF16),
            pltpu.VMEM((tok, width), BF16),
            pltpu.VMEM((tok, width), BF16),
            pltpu.VMEM((width, DH), BF16),
            pltpu.VMEM((row, sl, DH), BF16),
            pltpu.VMEM((nz, sl, DH), BF16),
            pltpu.VMEM((row, sl, DH), F32),
            pltpu.VMEM((row, sl, DH), BF16),
            pltpu.VMEM((width, DH), BF16),
            pltpu.VMEM((tok, DH), jnp.int32),
            pltpu.VMEM((heads, tok, DH), F32),
            pltpu.VMEM((ny, heads, tok, DH), BF16),
            pltpu.VMEM((ny, width, cols), BF16),
            pltpu.VMEM((tok, cols), F32),
            pltpu.VMEM((tok, cols), BF16),
            dma((4,)),
            dma((row,)), dma((row,)),
            dma((nz,)), dma((nz,)),
            dma((row,)), dma((row,)),
            dma((yh,)), dma((yh,)),
            dma((row // 2,)), dma((row // 2,)),
            dma((2, zh)), dma((2, zh)),
            dma((nz,)), dma((nz,)),
            dma((2, yh, heads)), dma((2, yh, heads)),
        ],
        compiler_params=pltpu.CompilerParams(collective_id=0, has_side_effects=True),
    )(queries, key_vectors, value_vectors, doc_lengths, norm_gain.reshape(1, width), out_weight)


def solution(mesh, row=ROW):
    nz, ny = mesh.shape["seq"] // row, mesh.shape["head"]
    return jax.shard_map(
        functools.partial(body, nz, row, ny),
        mesh=mesh,
        in_specs=(
            P("seq", "head"),
            P("seq", "head"),
            P("seq", "head"),
            P(),
            P("head"),
            P("head", None),
        ),
        out_specs=P("seq", "head"),
        check_vma=False,
    )
```

time: 195 us -> 65.3 us (0.33)
  waiting for transfers between devices: 151 us -> 0 us
  Pallas kernels: 0 us -> 61.9 us
  between operations: 16.9 us -> 0.01 us
  matrix products: 10.9 us -> 0 us
  other arithmetic: 10.2 us -> 0 us
  local copies, waits for them, and re-layouts: 6.53 us -> 3.11 us
    all_gather x1 -> x0, waiting for transfers between devices: 96.7 us -> none  [body(): shards = lax.all_gather(block_state[None], 'seq', axis=0, tiled=True)]
    pallas_call x0 -> x1, Pallas kernels: none -> 61.9 us  [body(): pl.pallas_call(functools.partial(layer_kernel, nz, row, ny), name='layer'...]
    reduce_scatter x1 -> x0, waiting for transfers between devices: 53.8 us -> none  [body(): lax.psum_scatter(partial_sum.astype(jnp.bfloat16), 'head', scatter_dimens...]
    dot_general x4 -> x0, matrix products: 10.9 us -> none  [the longest x1 4.31 us: body(): jnp.dot(normed, out_weight, preferred_element_type=jnp.float32)]
    reduce_sum x2 -> x0, other arithmetic: 6.61 us -> none  [the longest x1 5.87 us: body(): carried = jnp.sum(weights[:, None, None, None] * shards, axis=0)]
    unnamed x9 -> x1, local copies, waits for them, and re-layouts: 4.41 us -> 1.87 us
  transfers between devices with their start and end apart: 2 -> 0, of which waited for: 2 -> 0; matrix products, arithmetic and copies ran while one was open for 1% -> 0% of each run, Pallas kernels for 0% -> 0%
where the time goes in v1:
time: 65.3 us; the launch traced here: 65 us
  Pallas kernels  61.9 us (95%)
  local copies, waits for them, and re-layouts  3.11 us (5%)
    pallas_call x1, Pallas kernels, body(): pl.pallas_call(functools.partial(layer_kernel, nz, row, ny), name='layer'...  61.9 us
    unnamed x1, local copies, waits for them, and re-layouts  1.87 us

profile of v1, /device:TPU:1, one launch (start us, length us, event | category | flops | bytes accessed | tf_op | source)
XLA Modules:
  0.0 65.0 jit_solution(6814536266679557168)
XLA Ops:
  0.0 1.2 %reshape.3.gain = f32[1,384]{1,0:T(1,128)} reshape(f32[384]{0:T(512)} %param.10) | data formatting | bytes 3072 | tf_op jit(solution)/shard_map/reshape | solution.py:368
  1.2 61.9 %layer.1 = bf16[512,512]{1,0:T(8,128)(2,1)} custom-call(bf16[512,384]{1,0:T(8,128)(2,1)} %q_any.1, bf16[512,384]{1,0:T(8,128)(2,1)} %k_any.1, bf16[512,384]{1,0:T(8,128)(2,1)} %v_any.1, s32[16]{0:T(128)} %lens.1, f32[1,384]{1,0:T(1,128)} %reshape.3.gain, bf16[384,4096]{1,0:T(8,128)(2,1)} %w_any.1), custom_call_target="tpu_custom_call" | custom-call | tf_op jit(solution)/shard_map/layer/pallas_call | solution.py:330
  63.1 1.9 %copy.8 = bf16[512,512]{1,0:T(8,128)(2,1)} copy(bf16[512,512]{1,0:T(8,128)(2,1)} %layer.1) | data formatting | bytes 1048576

commit v2 on v1

--- a/solution.py
+++ b/solution.py
@@ -20,8 +20,8 @@
 
 def layer_kernel(
     nz, row, ny,
-    q_any, k_any, v_any, lens, gain, w_any, out_any,
-    q_ref, k_ref, v_ref, s_loc, s_in, r_in, crow, c_out, c_in, lo_ref, within, norm_all, wcol, acc, out_v,
+    q_any, k_any, v_any, lens_any, gain_any, w_any, out_v,
+    lens, gain, q_ref, k_ref, v_ref, s_loc, s_in, r_in, crow, c_out, c_in, lo_ref, within, norm_all, wcol, acc,
     load_sem, p1s, p1r, p2s, p2r, p3s, p3r, wys, wyr, wxs, wxr, wzs, wzr, wcs, wcr, ys, yr,
 ):
     tok, width = q_ref.shape
@@ -57,12 +57,20 @@
         return (seq, i)
 
     barrier = pltpu.get_barrier_semaphore()
-    peers = [row_dev((r + k) % row) for k in range(1, row)]
-    peers += [z_dev((z + k) % nz) for k in range(1, nz)]
-    peers += [y_dev((y + k) % ny) for k in range(1, ny)]
+    def far_first(n):
+        return sorted(range(1, n), key=lambda k: -min(k, n - k))
+
+    peers = [z_dev((z + k) % nz) for k in far_first(nz)]
+    peers += [y_dev((y + k) % ny) for k in far_first(ny)]
+    peers += [row_dev((r + k) % row) for k in far_first(row)]
+    r_in[...] = jnp.zeros_like(r_in)
     for peer in peers:
         pl.semaphore_signal(barrier, inc=1, device_id=peer, device_id_type=MESH)
 
+    small = [
+        pltpu.make_async_copy(lens_any, lens, load_sem.at[4]),
+        pltpu.make_async_copy(gain_any, gain, load_sem.at[5]),
+    ]
     loads = [
         pltpu.make_async_copy(k_any, k_ref, load_sem.at[0]),
         pltpu.make_async_copy(v_any, v_ref, load_sem.at[1]),
@@ -70,9 +78,10 @@
         pltpu.make_async_copy(
             w_any.at[:, pl.ds(pl.multiple_of(y * cols, 128), cols)], wcol.at[0], load_sem.at[3]),
     ]
-    for load in loads:
+    for load in small[:1] + loads + small[1:]:
         load.start()
 
+    small[0].wait()
     bounds, total = [], jnp.int32(0)
     for d in range(lens.shape[0]):
         total = total + lens[d]
@@ -110,7 +119,7 @@
     def part(i):
         return pl.ds(pl.multiple_of(i * sl, 16), sl)
 
-    for k in range(1, row):
+    for k in far_first(row):
         i = (r + k) % row
         send(s_loc.at[part(i)], s_in.at[r], p1s.at[k], p1r.at[k], row_dev(i))
 
@@ -155,8 +164,34 @@
     state = [s_in[j].astype(F32) for j in range(row)]
     row_sum = functools.reduce(jnp.add, [w_row_sum[j] * state[j] for j in range(row)])
     r_in[z] = row_sum.astype(BF16)
+
+    def p2_copy(k, i):
+        return remote(r_in.at[i], r_in.at[i], p2s.at[k], p2r.at[k], z_dev((z + k) % nz))
+
+    for k in far_first(nz):
+        @pl.when(z + k < nz)
+        def _():
+            p2_copy(k, z).start()
+
+    for i in range(row):
+        total = jnp.zeros((sl, DH), F32)
+        for j in range(i):
+            total = total + flag((first + j + 1) * tok > row_start[i]) * state[j]
+        crow[i] = total
+    attend(1)
+
     for k in range(1, nz):
-        send(r_in.at[z], r_in.at[z], p2s.at[k], p2r.at[k], z_dev((z + k) % nz))
+        @pl.when(z >= k)
+        def _():
+            p2_copy(k, (z + nz - k) % nz).wait_recv()
+
+    past = functools.reduce(jnp.add, [w_rows[i] * r_in[i].astype(F32) for i in range(nz)])
+    for i in range(row):
+        c_out[i] = (crow[i] + w_past[i] * past).astype(BF16)
+    for k in far_first(row):
+        i = (r + k) % row
+        send(c_out.at[i], c_in.at[part(r)], p3s.at[k], p3r.at[k], row_dev(i))
+    c_in[part(r), :] = c_out[r]
 
     rels = pl.ds(first_rel, yh)
     for i in range(yh):
@@ -164,35 +199,11 @@
         remote(
             w_any.at[z_rows, pl.ds(0, xc)], wcol.at[rel, z_rows, x_cols],
             wys.at[i], wyr.at[i], y_dev((y + rel) % ny)).wait_recv()
-    for k in range(1, nx):
+    for k in far_first(nx):
         block = wcol.at[rels, z_rows, x_cols]
         send(block, block, wxs.at[k], wxr.at[k], row_dev((x + k) % nx * 2 + c))
 
-    for i in range(row):
-        total = jnp.zeros((sl, DH), F32)
-        for j in range(i):
-            total = total + flag((first + j + 1) * tok > row_start[i]) * state[j]
-        crow[i] = total
-    attend(1)
-
-    for k in range(1, nz):
-        i = (z + nz - k) % nz
-        remote(r_in.at[i], r_in.at[i], p2s.at[k], p2r.at[k], z_dev(i)).wait_recv()
-
-    past = functools.reduce(jnp.add, [w_rows[i] * r_in[i].astype(F32) for i in range(nz)])
-    for i in range(row):
-        c_out[i] = (crow[i] + w_past[i] * past).astype(BF16)
-    for k in range(1, row):
-        i = (r + k) % row
-        send(c_out.at[i], c_in.at[part(r)], p3s.at[k], p3r.at[k], row_dev(i))
-    c_in[part(r), :] = c_out[r]
-
     attend(2)
-
-    for k in range(1, nx):
-        i = (x + nx - k) % nx
-        block = wcol.at[rels, z_rows, pl.ds(pl.multiple_of(i * xc, 128), xc)]
-        remote(block, block, wxs.at[k], wxr.at[k], row_dev(i * 2 + c)).wait_recv()
 
     def z_block(i, first, count):
         return wcol.at[pl.ds(first, count), pl.ds(pl.multiple_of(i * wr, 16), wr), :]
@@ -234,8 +245,6 @@
             block = z_block((z + n) % nz, twin_rels, yh - 1)
             remote(block, block, wcs.at[n], wcr.at[n], twin).wait_recv()
 
-    z_step(0)
-
     for k in range(1, row):
         j = (r + row - k) % row
         remote(c_out.at[j], c_in.at[part(j)], p3s.at[k], p3r.at[k], row_dev(j)).wait_recv()
@@ -258,10 +267,11 @@
         for way in ways:
             remote(*y_copy(way, d - 1, h, False)).wait_recv()
 
+    small[1].wait()
     for h in range(heads):
         hs = slice(h * DH, (h + 1) * DH)
         carried = c_in[hs, :]
-        scale = gain[:, hs]
+        scale = jnp.broadcast_to(gain[hs][None, :], (tb, DH))
         for b in range(2):
             ts = slice(b * tb, (b + 1) * tb)
             term = dot(q_ref[ts, hs], carried)
@@ -269,6 +279,13 @@
             square_mean = jnp.mean(mixture * mixture, axis=-1, keepdims=True)
             norm_all[0, h, ts, :] = (mixture * lax.rsqrt(square_mean + 1e-06) * scale).astype(BF16)
         y_send(0, h)
+
+    for k in range(1, nx):
+        i = (x + nx - k) % nx
+        block = wcol.at[rels, z_rows, pl.ds(pl.multiple_of(i * xc, 128), xc)]
+        remote(block, block, wxs.at[k], wxr.at[k], row_dev(i * 2 + c)).wait_recv()
+
+    z_step(0)
 
     def project(rel, start=False):
         for b in range(2):
@@ -310,13 +327,12 @@
                 acc[ts, :] = total
             else:
                 out_v[ts, :] = total.astype(BF16)
-                load_sem_way = load_sem.at[way]
-                pltpu.make_async_copy(out_v.at[ts], out_any.at[ts], load_sem_way).start()
     for copy in sends:
         copy.wait_send()
-    for way in range(2):
-        ts = slice(way * tb, (way + 1) * tb)
-        pltpu.make_async_copy(out_v.at[ts], out_any.at[ts], load_sem.at[way]).wait()
+    for k in range(1, nz):
+        @pl.when(z + k < nz)
+        def _():
+            p2_copy(k, z).wait_send()
 
 
 def body(nz, row, ny, queries, key_vectors, value_vectors, doc_lengths, norm_gain, out_weight):
@@ -330,15 +346,12 @@
     return pl.pallas_call(
         functools.partial(layer_kernel, nz, row, ny),
         name="layer",
-        out_shape=jax.ShapeDtypeStruct((tok, cols), BF16),
-        in_specs=[
-            any_spec, any_spec, any_spec,
-            pl.BlockSpec(memory_space=pltpu.SMEM),
-            pl.BlockSpec(memory_space=pltpu.VMEM),
-            any_spec,
-        ],
-        out_specs=any_spec,
+        out_shape=pltpu.VMEM((tok, cols), BF16),
+        in_specs=[any_spec] * 6,
+        out_specs=pl.BlockSpec(memory_space=pltpu.VMEM),
         scratch_shapes=[
+            pltpu.SMEM(doc_lengths.shape, jnp.int32),
+            pltpu.VMEM((width,), F32),
             pltpu.VMEM((tok, width), BF16),
             pltpu.VMEM((tok, width), BF16),
             pltpu.VMEM((tok, width), BF16),
@@ -353,8 +366,7 @@
             pltpu.VMEM((ny, heads, tok, DH), BF16),
             pltpu.VMEM((ny, width, cols), BF16),
             pltpu.VMEM((tok, cols), F32),
-            pltpu.VMEM((tok, cols), BF16),
-            dma((4,)),
+            dma((6,)),
             dma((row,)), dma((row,)),
             dma((nz,)), dma((nz,)),
             dma((row,)), dma((row,)),
@@ -365,7 +377,7 @@
             dma((2, yh, heads)), dma((2, yh, heads)),
         ],
         compiler_params=pltpu.CompilerParams(collective_id=0, has_side_effects=True),
-    )(queries, key_vectors, value_vectors, doc_lengths, norm_gain.reshape(1, width), out_weight)
+    )(queries, key_vectors, value_vectors, doc_lengths, norm_gain, out_weight)
 
 
 def solution(mesh, row=ROW):

time: 65.3 us -> 61.4 us (0.940)
  local copies, waits for them, and re-layouts: 3.11 us -> 0.8 us
  Pallas kernels: 61.9 us -> 60.5 us
    pallas_call x1, Pallas kernels: 61.9 us -> 60.5 us  [body(): pl.pallas_call(functools.partial(layer_kernel, nz, row, ny), name='layer'...]
    reshape x1 -> x0, local copies, waits for them, and re-layouts: 1.24 us -> none  [body(): norm_gain.reshape(1, width)]
    unnamed x1, local copies, waits for them, and re-layouts: 1.87 us -> 0.8 us
where the time goes in v2:
time: 61.4 us; the launch traced here: 61.3 us
  Pallas kernels  60.5 us (99%)
  local copies, waits for them, and re-layouts  0.8 us (1%)
    pallas_call x1, Pallas kernels, body(): pl.pallas_call(functools.partial(layer_kernel, nz, row, ny), name='layer'...  60.5 us

profile of v2, /device:TPU:1, one launch (start us, length us, event | category | flops | bytes accessed | tf_op | source)
XLA Modules:
  0.0 61.3 jit_solution(18179998590123570278)
XLA Ops:
  0.0 60.5 %layer.1 = bf16[512,512]{1,0:T(8,128)(2,1)S(1)} custom-call(bf16[512,384]{1,0:T(8,128)(2,1)} %q_any.1, bf16[512,384]{1,0:T(8,128)(2,1)} %k_any.1, bf16[512,384]{1,0:T(8,128)(2,1)} %v_any.1, s32[16]{0:T(128)} %lens_any.1, f32[384]{0:T(512)} %gain_any.1, bf16[384,4096]{1,0:T(8,128)(2,1)} %w_any.1), custom_call_target="tpu_custom_call" | custom-call | tf_op jit(solution)/shard_map/layer/pallas_call | solution.py:346
  60.5 0.8 %copy.8 = bf16[512,512]{1,0:T(8,128)(2,1)} copy(bf16[512,512]{1,0:T(8,128)(2,1)S(1)} %layer.1) | data formatting | bytes 1048576

commit v3 on v2

--- a/solution.py
+++ b/solution.py
@@ -22,16 +22,14 @@
     nz, row, ny,
     q_any, k_any, v_any, lens_any, gain_any, w_any, out_v,
     lens, gain, q_ref, k_ref, v_ref, s_loc, s_in, r_in, crow, c_out, c_in, lo_ref, within, norm_all, wcol, acc,
-    load_sem, p1s, p1r, p2s, p2r, p3s, p3r, wys, wyr, wxs, wxr, wzs, wzr, wcs, wcr, ys, yr,
+    load_sem, p1s, p1r, p2s, p2r, p3s, p3r, wys, wyr, wzs, wzr, wcs, wcr, ys, yr,
 ):
     tok, width = q_ref.shape
     heads = width // DH
     cols = out_v.shape[1]
-    nx = row // 2
     yh, zh = ny // 2, nz // 2
-    sl = width // row
+    sl = DH // row
     wr = width // nz
-    xc = cols // nx
     seq, y = lax.axis_index("seq"), lax.axis_index("head")
     z, r = seq // row, seq % row
     x, c = r // 2, r % 2
@@ -46,6 +44,9 @@
         copy = remote(*args)
         copy.start()
         sends.append(copy)
+
+    def wait_bytes(ref, sem):
+        pltpu.make_async_copy(ref, ref, sem).wait()
 
     def row_dev(i):
         return (z * row + i, y)
@@ -112,28 +113,29 @@
     for h in range(heads):
         hs = slice(h * DH, (h + 1) * DH)
         key = (k_ref[:, hs].astype(F32) * keep).astype(BF16)
-        s_loc[hs, :] = dot(key, v_ref[:, hs], ((0,), (0,))).astype(BF16)
+        s_loc[h] = dot(key, v_ref[:, hs], ((0,), (0,))).astype(BF16)
 
     pl.semaphore_wait(barrier, len(peers))
 
     def part(i):
         return pl.ds(pl.multiple_of(i * sl, 16), sl)
 
-    for k in far_first(row):
-        i = (r + k) % row
-        send(s_loc.at[part(i)], s_in.at[r], p1s.at[k], p1r.at[k], row_dev(i))
+    for h in range(heads):
+        for k in far_first(row):
+            i = (r + k) % row
+            remote(s_loc.at[h, part(i)], s_in.at[h, r], p1s.at[h], p1r.at[h], row_dev(i)).start()
 
     first_rel = 1 + (yh - 1) * c
     z_rows = pl.ds(pl.multiple_of(z * wr, 16), wr)
-    x_cols = pl.ds(pl.multiple_of(x * xc, 128), xc)
     for i in range(yh):
         rel = first_rel + i
         plane = (y + ny - rel) % ny
-        send(
-            w_any.at[z_rows, pl.ds(pl.multiple_of(plane * cols + x * xc, 128), xc)],
-            wcol.at[rel, z_rows, x_cols], wys.at[i], wyr.at[i], y_dev(plane))
-
-    s_in[r] = s_loc[part(r), :]
+        remote(
+            w_any.at[z_rows, pl.ds(pl.multiple_of(plane * cols, 128), cols)],
+            wcol.at[rel, z_rows, :], wys, wyr, y_dev(plane)).start()
+
+    for h in range(heads):
+        s_in[h, r] = s_loc[h, part(r), :]
     lo = jnp.zeros((tok, DH), jnp.int32) - offset
     for bound in bounds:
         lo = jnp.where(rows >= bound - offset, bound - offset, lo)
@@ -157,97 +159,77 @@
 
     attend(0)
 
-    for k in range(1, row):
-        j = (r + row - k) % row
-        remote(s_loc.at[part(j)], s_in.at[j], p1s.at[k], p1r.at[k], row_dev(j)).wait_recv()
-
-    state = [s_in[j].astype(F32) for j in range(row)]
-    row_sum = functools.reduce(jnp.add, [w_row_sum[j] * state[j] for j in range(row)])
-    r_in[z] = row_sum.astype(BF16)
-
-    def p2_copy(k, i):
-        return remote(r_in.at[i], r_in.at[i], p2s.at[k], p2r.at[k], z_dev((z + k) % nz))
-
-    for k in far_first(nz):
-        @pl.when(z + k < nz)
-        def _():
-            p2_copy(k, z).start()
-
-    for i in range(row):
-        total = jnp.zeros((sl, DH), F32)
-        for j in range(i):
-            total = total + flag((first + j + 1) * tok > row_start[i]) * state[j]
-        crow[i] = total
+    def p2_copy(h, k, i):
+        return remote(
+            r_in.at[h, i], r_in.at[h, i], p2s.at[h, k], p2r.at[h, k], z_dev((z + k) % nz))
+
+    others = pl.ds(0, row - 1)
+    for h in range(heads):
+        wait_bytes(s_in.at[h, others], p1r.at[h])
+        row_sum = functools.reduce(
+            jnp.add, [w_row_sum[j] * s_in[h, j].astype(F32) for j in range(row)])
+        r_in[h, z] = row_sum.astype(BF16)
+        for k in far_first(nz):
+            @pl.when(z + k < nz)
+            def _():
+                p2_copy(h, k, z).start()
+
+    w_own = {
+        (i, j): flag((first + j + 1) * tok > row_start[i]) for i in range(row) for j in range(i)}
+    for h in range(heads):
+        state = [s_in[h, j].astype(F32) for j in range(row)]
+        for i in range(row):
+            total = jnp.zeros((sl, DH), F32)
+            for j in range(i):
+                total = total + w_own[i, j] * state[j]
+            crow[h, i] = total
     attend(1)
 
-    for k in range(1, nz):
-        @pl.when(z >= k)
-        def _():
-            p2_copy(k, (z + nz - k) % nz).wait_recv()
-
-    past = functools.reduce(jnp.add, [w_rows[i] * r_in[i].astype(F32) for i in range(nz)])
-    for i in range(row):
-        c_out[i] = (crow[i] + w_past[i] * past).astype(BF16)
-    for k in far_first(row):
-        i = (r + k) % row
-        send(c_out.at[i], c_in.at[part(r)], p3s.at[k], p3r.at[k], row_dev(i))
-    c_in[part(r), :] = c_out[r]
-
-    rels = pl.ds(first_rel, yh)
-    for i in range(yh):
-        rel = first_rel + i
-        remote(
-            w_any.at[z_rows, pl.ds(0, xc)], wcol.at[rel, z_rows, x_cols],
-            wys.at[i], wyr.at[i], y_dev((y + rel) % ny)).wait_recv()
-    for k in far_first(nx):
-        block = wcol.at[rels, z_rows, x_cols]
-        send(block, block, wxs.at[k], wxr.at[k], row_dev((x + k) % nx * 2 + c))
+    for h in range(heads):
+        for k in range(1, nz):
+            @pl.when(z >= k)
+            def _():
+                p2_copy(h, k, (z + nz - k) % nz).wait_recv()
+        past = functools.reduce(
+            jnp.add, [w_rows[i] * r_in[h, i].astype(F32) for i in range(nz)])
+        for i in range(row):
+            c_out[h, i] = (crow[h, i] + w_past[i] * past).astype(BF16)
+        for k in far_first(row):
+            i = (r + k) % row
+            remote(c_out.at[h, i], c_in.at[h, part(r)], p3s.at[h], p3r.at[h], row_dev(i)).start()
+        c_in[h, part(r), :] = c_out[h, r]
 
     attend(2)
 
     def z_block(i, first, count):
         return wcol.at[pl.ds(first, count), pl.ds(pl.multiple_of(i * wr, 16), wr), :]
 
-    def z_copy(way, d, starting):
+    def z_copy(way, d, half, starting):
         step = 1 if way == 0 else nz - 1
         away = d if starting else d + 1
         owner = (z + away * (nz - step)) % nz
-        if d < zh - 1:
-            block = z_block(owner, first_rel, yh)
-        elif way == 0:
-            block = z_block(owner, first_rel, yh // 2)
-        else:
-            block = z_block(owner, first_rel + yh // 2, yh - yh // 2)
-        return block, block, wzs.at[way, d], wzr.at[way, d], z_dev((z + step) % nz)
+        count = yh // 2 if half == 0 else yh - yh // 2
+        block = z_block(owner, first_rel + half * (yh // 2), count)
+        return block, block, wzs.at[way, half, d], wzr.at[way, half, d], z_dev((z + step) % nz)
 
     own_rels, twin_rels = 1 + yh * c, 1 + yh * (1 - c)
     twin = row_dev(x * 2 + (1 - c))
 
-    def to_twin(i, n):
+    def to_twin(i):
         block = z_block(i, own_rels, yh - 1)
-        send(block, block, wcs.at[n], wcr.at[n], twin)
-
-    def z_step(d):
-        if d > 0:
-            for way in range(2):
-                remote(*z_copy(way, d - 1, False)).wait_recv()
-        if d < zh:
-            for way in range(2):
-                send(*z_copy(way, d, True))
-        if d == 0 or d == zh:
-            to_twin((z + d) % nz, d)
-        else:
-            to_twin((z + d) % nz, d)
-            to_twin((z + nz - d) % nz, nz - d)
-
-    def twin_wait():
-        for n in range(nz):
-            block = z_block((z + n) % nz, twin_rels, yh - 1)
-            remote(block, block, wcs.at[n], wcr.at[n], twin).wait_recv()
-
-    for k in range(1, row):
-        j = (r + row - k) % row
-        remote(c_out.at[j], c_in.at[part(j)], p3s.at[k], p3r.at[k], row_dev(j)).wait_recv()
+        remote(block, block, wcs, wcr, twin).start()
+
+    def z_step(d, half):
+        for way in range(2):
+            if d > 0 and (d < zh or way == half):
+                remote(*z_copy(way, d - 1, half, False)).wait_recv()
+        for way in range(2):
+            if d < zh - 1 or (d == zh - 1 and way == half):
+                send(*z_copy(way, d, half, True))
+        if half == 1:
+            to_twin((z + d) % nz)
+            if 0 < d < zh:
+                to_twin((z + nz - d) % nz)
 
     def y_copy(way, d, h, starting):
         slot = (ny - d) % ny if way == 0 else d
@@ -270,7 +252,8 @@
     small[1].wait()
     for h in range(heads):
         hs = slice(h * DH, (h + 1) * DH)
-        carried = c_in[hs, :]
+        wait_bytes(c_in.at[h, pl.ds(0, sl * (row - 1))], p3r.at[h])
+        carried = c_in[h]
         scale = jnp.broadcast_to(gain[hs][None, :], (tb, DH))
         for b in range(2):
             ts = slice(b * tb, (b + 1) * tb)
@@ -280,13 +263,6 @@
             norm_all[0, h, ts, :] = (mixture * lax.rsqrt(square_mean + 1e-06) * scale).astype(BF16)
         y_send(0, h)
 
-    for k in range(1, nx):
-        i = (x + nx - k) % nx
-        block = wcol.at[rels, z_rows, pl.ds(pl.multiple_of(i * xc, 128), xc)]
-        remote(block, block, wxs.at[k], wxr.at[k], row_dev(i * 2 + c)).wait_recv()
-
-    z_step(0)
-
     def project(rel, start=False):
         for b in range(2):
             ts = slice(b * tb, (b + 1) * tb)
@@ -300,21 +276,37 @@
 
     loads[3].wait()
     project(0, True)
-    z_left = list(range(1, zh + 1))
-    n = 0
-    for d in range(1, yh):
-        if d == yh - 1:
-            while z_left:
-                z_step(z_left.pop(0))
-            twin_wait()
-            for e in range(1, d):
+    y_events = [(d, h) for d in range(1, yh) for h in range(heads)]
+    z_events = [(d, half) for d in range(1, zh + 1) for half in range(2)]
+    z_after = [min(2 + m * 3 // 4, len(y_events) - 2) for m in range(len(z_events))]
+    for n, (d, h) in enumerate(y_events):
+        y_step(d, h)
+        if n == 0:
+            wait_bytes(z_block(z, first_rel, yh), wyr)
+            z_step(0, 0)
+            z_step(0, 1)
+        for after, event in zip(z_after, z_events):
+            if after == n:
+                z_step(*event)
+        if n == 2:
+            for h2 in range(heads):
+                wait_bytes(s_in.at[h2, others], p1s.at[h2])
+                wait_bytes(s_in.at[h2, others], p3s.at[h2])
+                for k in range(1, nz):
+                    @pl.when(z + k < nz)
+                    def _():
+                        p2_copy(h2, k, z).wait_send()
+            wait_bytes(z_block(z, first_rel, yh), wys)
+        if n == len(y_events) // 2:
+            early = len(sends)
+        if n == len(y_events) - 1:
+            wait_bytes(wcol.at[pl.ds(twin_rels, yh - 1)], wcr)
+            wait_bytes(wcol.at[pl.ds(own_rels, yh - 1)], wcs)
+            for copy in sends[:early]:
+                copy.wait_send()
+            for e in range(1, yh - 1):
                 project(e)
                 project(ny - e)
-        for h in range(heads):
-            y_step(d, h)
-            n += 1
-            if n in (1, 3, 5, 6) and z_left:
-                z_step(z_left.pop(0))
     project(yh - 1)
     project(yh + 1)
     for h in range(heads):
@@ -327,12 +319,8 @@
                 acc[ts, :] = total
             else:
                 out_v[ts, :] = total.astype(BF16)
-    for copy in sends:
+    for copy in sends[early:]:
         copy.wait_send()
-    for k in range(1, nz):
-        @pl.when(z + k < nz)
-        def _():
-            p2_copy(k, z).wait_send()
 
 
 def body(nz, row, ny, queries, key_vectors, value_vectors, doc_lengths, norm_gain, out_weight):
@@ -340,7 +328,7 @@
     heads = width // DH
     cols = out_weight.shape[1] // ny
     yh, zh = ny // 2, nz // 2
-    sl = width // row
+    sl = DH // row
     dma = pltpu.SemaphoreType.DMA
     any_spec = pl.BlockSpec(memory_space=pl.ANY)
     return pl.pallas_call(
@@ -355,25 +343,24 @@
             pltpu.VMEM((tok, width), BF16),
             pltpu.VMEM((tok, width), BF16),
             pltpu.VMEM((tok, width), BF16),
-            pltpu.VMEM((width, DH), BF16),
-            pltpu.VMEM((row, sl, DH), BF16),
-            pltpu.VMEM((nz, sl, DH), BF16),
-            pltpu.VMEM((row, sl, DH), F32),
-            pltpu.VMEM((row, sl, DH), BF16),
-            pltpu.VMEM((width, DH), BF16),
+            pltpu.VMEM((heads, DH, DH), BF16),
+            pltpu.VMEM((heads, row, sl, DH), BF16),
+            pltpu.VMEM((heads, nz, sl, DH), BF16),
+            pltpu.VMEM((heads, row, sl, DH), F32),
+            pltpu.VMEM((heads, row, sl, DH), BF16),
+            pltpu.VMEM((heads, DH, DH), BF16),
             pltpu.VMEM((tok, DH), jnp.int32),
             pltpu.VMEM((heads, tok, DH), F32),
             pltpu.VMEM((ny, heads, tok, DH), BF16),
             pltpu.VMEM((ny, width, cols), BF16),
             pltpu.VMEM((tok, cols), F32),
             dma((6,)),
-            dma((row,)), dma((row,)),
-            dma((nz,)), dma((nz,)),
-            dma((row,)), dma((row,)),
-            dma((yh,)), dma((yh,)),
-            dma((row // 2,)), dma((row // 2,)),
-            dma((2, zh)), dma((2, zh)),
-            dma((nz,)), dma((nz,)),
+            dma((heads,)), dma((heads,)),
+            dma((heads, nz)), dma((heads, nz)),
+            dma((heads,)), dma((heads,)),
+            dma(()), dma(()),
+            dma((2, 2, zh)), dma((2, 2, zh)),
+            dma(()), dma(()),
             dma((2, yh, heads)), dma((2, yh, heads)),
         ],
         compiler_params=pltpu.CompilerParams(collective_id=0, has_side_effects=True),

time: 61.4 us -> 58.3 us (0.950)
  Pallas kernels: 60.5 us -> 57.3 us
    pallas_call x1, Pallas kernels: 60.5 us -> 57.3 us  [body(): pl.pallas_call(functools.partial(layer_kernel, nz, row, ny), name='layer'...]
where the time goes in v3:
time: 58.3 us; the launch traced here: 58.1 us
  Pallas kernels  57.3 us (98%)
  local copies, waits for them, and re-layouts  0.8 us (1%)
    pallas_call x1, Pallas kernels, body(): pl.pallas_call(functools.partial(layer_kernel, nz, row, ny), name='layer'...  57.3 us

profile of v3, /device:TPU:1, one launch (start us, length us, event | category | flops | bytes accessed | tf_op | source)
XLA Modules:
  0.0 58.1 jit_solution(2751966648152957167)
XLA Ops:
  0.0 57.3 %layer.1 = bf16[512,512]{1,0:T(8,128)(2,1)S(1)} custom-call(bf16[512,384]{1,0:T(8,128)(2,1)} %q_any.1, bf16[512,384]{1,0:T(8,128)(2,1)} %k_any.1, bf16[512,384]{1,0:T(8,128)(2,1)} %v_any.1, s32[16]{0:T(128)} %lens_any.1, f32[384]{0:T(512)} %gain_any.1, bf16[384,4096]{1,0:T(8,128)(2,1)} %w_any.1), custom_call_target="tpu_custom_call" | custom-call | tf_op jit(solution)/shard_map/layer/pallas_call | solution.py:334
  57.3 0.8 %copy.8 = bf16[512,512]{1,0:T(8,128)(2,1)} copy(bf16[512,512]{1,0:T(8,128)(2,1)S(1)} %layer.1) | data formatting | bytes 1048576

commit v4 on v3

--- a/solution.py
+++ b/solution.py
@@ -22,7 +22,7 @@
     nz, row, ny,
     q_any, k_any, v_any, lens_any, gain_any, w_any, out_v,
     lens, gain, q_ref, k_ref, v_ref, s_loc, s_in, r_in, crow, c_out, c_in, lo_ref, within, norm_all, wcol, acc,
-    load_sem, p1s, p1r, p2s, p2r, p3s, p3r, wys, wyr, wzs, wzr, wcs, wcr, ys, yr,
+    load_sem, p1s, p1r, p2s, p2r, p3s, p3r, wys, wyr, wzs, wzr, wcs, wcr, ys, yr, z_level, y_level,
 ):
     tok, width = q_ref.shape
     heads = width // DH
@@ -61,9 +61,9 @@
     def far_first(n):
         return sorted(range(1, n), key=lambda k: -min(k, n - k))
 
-    peers = [z_dev((z + k) % nz) for k in far_first(nz)]
-    peers += [y_dev((y + k) % ny) for k in far_first(ny)]
-    peers += [row_dev((r + k) % row) for k in far_first(row)]
+    z_near = [z_dev((z + 1) % nz), z_dev((z + nz - 1) % nz)]
+    y_near = [y_dev((y + 1) % ny), y_dev((y + ny - 1) % ny)]
+    peers = z_near + y_near + [row_dev((r + k) % row) for k in far_first(row)]
     r_in[...] = jnp.zeros_like(r_in)
     for peer in peers:
         pl.semaphore_signal(barrier, inc=1, device_id=peer, device_id_type=MESH)
@@ -117,6 +117,15 @@
 
     pl.semaphore_wait(barrier, len(peers))
 
+    def tell(near, level):
+        for peer in near:
+            pl.semaphore_signal(level, inc=1, device_id=peer, device_id_type=MESH)
+
+    def relay(near, levels, n, last):
+        pl.semaphore_wait(levels.at[n], 2)
+        if n < last - 1:
+            tell(near, levels.at[n + 1])
+
     def part(i):
         return pl.ds(pl.multiple_of(i * sl, 16), sl)
 
@@ -127,13 +136,8 @@
 
     first_rel = 1 + (yh - 1) * c
     z_rows = pl.ds(pl.multiple_of(z * wr, 16), wr)
-    for i in range(yh):
-        rel = first_rel + i
-        plane = (y + ny - rel) % ny
-        remote(
-            w_any.at[z_rows, pl.ds(pl.multiple_of(plane * cols, 128), cols)],
-            wcol.at[rel, z_rows, :], wys, wyr, y_dev(plane)).start()
-
+    tell(z_near, z_level.at[0])
+    tell(y_near, y_level.at[0])
     for h in range(heads):
         s_in[h, r] = s_loc[h, part(r), :]
     lo = jnp.zeros((tok, DH), jnp.int32) - offset
@@ -157,7 +161,10 @@
             scores = jnp.where(allowed, scores, 0.0).astype(BF16)
             within[h, ts, :] = dot(scores, v_ref[:upto, hs])
 
+    relay(z_near, z_level, 0, zh - 1)
     attend(0)
+    for n in range(1, zh - 1):
+        relay(z_near, z_level, n, zh - 1)
 
     def p2_copy(h, k, i):
         return remote(
@@ -174,6 +181,14 @@
             def _():
                 p2_copy(h, k, z).start()
 
+    for n in range(yh - 1):
+        relay(y_near, y_level, n, yh - 1)
+    for i in range(yh):
+        rel = first_rel + i
+        plane = (y + ny - rel) % ny
+        remote(
+            w_any.at[z_rows, pl.ds(pl.multiple_of(plane * cols, 128), cols)],
+            wcol.at[rel, z_rows, :], wys, wyr, y_dev(plane)).start()
     w_own = {
         (i, j): flag((first + j + 1) * tok > row_start[i]) for i in range(row) for j in range(i)}
     for h in range(heads):
@@ -274,17 +289,16 @@
         y_wait(d, h)
         y_send(d, h)
 
+    wait_bytes(z_block(z, first_rel, yh), wyr)
+    z_step(0, 0)
+    z_step(0, 1)
     loads[3].wait()
     project(0, True)
     y_events = [(d, h) for d in range(1, yh) for h in range(heads)]
     z_events = [(d, half) for d in range(1, zh + 1) for half in range(2)]
-    z_after = [min(2 + m * 3 // 4, len(y_events) - 2) for m in range(len(z_events))]
+    z_after = [min(m, len(y_events) - 3) for m in range(len(z_events))]
     for n, (d, h) in enumerate(y_events):
         y_step(d, h)
-        if n == 0:
-            wait_bytes(z_block(z, first_rel, yh), wyr)
-            z_step(0, 0)
-            z_step(0, 1)
         for after, event in zip(z_after, z_events):
             if after == n:
                 z_step(*event)
@@ -362,6 +376,8 @@
             dma((2, 2, zh)), dma((2, 2, zh)),
             dma(()), dma(()),
             dma((2, yh, heads)), dma((2, yh, heads)),
+            pltpu.SemaphoreType.REGULAR((zh - 1,)),
+            pltpu.SemaphoreType.REGULAR((yh - 1,)),
         ],
         compiler_params=pltpu.CompilerParams(collective_id=0, has_side_effects=True),
     )(queries, key_vectors, value_vectors, doc_lengths, norm_gain, out_weight)

time: 58.3 us -> 60.9 us (1.045)
  Pallas kernels: 57.3 us -> 59.9 us
    pallas_call x1, Pallas kernels: 57.3 us -> 59.9 us  [body(): pl.pallas_call(functools.partial(layer_kernel, nz, row, ny), name='layer'...]
where the time goes in v4:
time: 60.9 us; the launch traced here: 60.7 us
  Pallas kernels  59.9 us (98%)
  local copies, waits for them, and re-layouts  0.8 us (1%)
    pallas_call x1, Pallas kernels, body(): pl.pallas_call(functools.partial(layer_kernel, nz, row, ny), name='layer'...  59.9 us

profile of v4, /device:TPU:1, one launch (start us, length us, event | category | flops | bytes accessed | tf_op | source)
XLA Modules:
  0.0 60.7 jit_solution(12251524988862950272)
XLA Ops:
  0.0 59.9 %layer.1 = bf16[512,512]{1,0:T(8,128)(2,1)S(1)} custom-call(bf16[512,384]{1,0:T(8,128)(2,1)} %q_any.1, bf16[512,384]{1,0:T(8,128)(2,1)} %k_any.1, bf16[512,384]{1,0:T(8,128)(2,1)} %v_any.1, s32[16]{0:T(128)} %lens_any.1, f32[384]{0:T(512)} %gain_any.1, bf16[384,4096]{1,0:T(8,128)(2,1)} %w_any.1), custom_call_target="tpu_custom_call" | custom-call | tf_op jit(solution)/shard_map/layer/pallas_call | solution.py:348
  59.9 0.8 %copy.8 = bf16[512,512]{1,0:T(8,128)(2,1)} copy(bf16[512,512]{1,0:T(8,128)(2,1)S(1)} %layer.1) | data formatting | bytes 1048576

commit v5 on v3

--- a/solution.py
+++ b/solution.py
@@ -21,8 +21,8 @@
 def layer_kernel(
     nz, row, ny,
     q_any, k_any, v_any, lens_any, gain_any, w_any, out_v,
-    lens, gain, q_ref, k_ref, v_ref, s_loc, s_in, r_in, crow, c_out, c_in, lo_ref, within, norm_all, wcol, acc,
-    load_sem, p1s, p1r, p2s, p2r, p3s, p3r, wys, wyr, wzs, wzr, wcs, wcr, ys, yr,
+    lens, gain, q_ref, k_ref, v_ref, s_loc, s_in, r_in, crow, c_out, c_in, lo_ref, within, within_0, q_near, in_near, c_near, g_below, g_above, norm_all, wcol, acc,
+    load_sem, p1s, p1r, p2s, p2r, p3s, p3r, wys, wyr, wzs, wzr, wcs, wcr, ys, yr, es, er,
 ):
     tok, width = q_ref.shape
     heads = width // DH
@@ -125,10 +125,31 @@
             i = (r + k) % row
             remote(s_loc.at[h, part(i)], s_in.at[h, r], p1s.at[h], p1r.at[h], row_dev(i)).start()
 
+    y_near = (y_dev((y + 1) % ny), y_dev((y + ny - 1) % ny))
+    g_near = (g_below, g_above)
+
+    def near_copy(way, kind):
+        src, dst = (
+            (q_ref.at[:, pl.ds(0, DH)], q_near.at[way]),
+            (gain, g_near[way]),
+            (within_0, in_near.at[way]),
+            (c_in.at[0], c_near.at[way]),
+        )[kind]
+        return remote(src, dst, es.at[way, kind], er.at[way, kind], y_near[way])
+
+    def near_send(kind):
+        for way in range(2):
+            near_copy(way, kind).start()
+
+    loads[2].wait()
+    near_send(0)
+    small[1].wait()
+    near_send(1)
+
     first_rel = 1 + (yh - 1) * c
     z_rows = pl.ds(pl.multiple_of(z * wr, 16), wr)
     for i in range(yh):
-        rel = first_rel + i
+        rel = yh + i * (2 * c - 1)
         plane = (y + ny - rel) % ny
         remote(
             w_any.at[z_rows, pl.ds(pl.multiple_of(plane * cols, 128), cols)],
@@ -140,7 +161,6 @@
     for bound in bounds:
         lo = jnp.where(rows >= bound - offset, bound - offset, lo)
     lo_ref[...] = lo
-    loads[2].wait()
 
     tb = tok // 2
 
@@ -158,6 +178,8 @@
             within[h, ts, :] = dot(scores, v_ref[:upto, hs])
 
     attend(0)
+    within_0[...] = within[0].astype(BF16)
+    near_send(2)
 
     def p2_copy(h, k, i):
         return remote(
@@ -249,19 +271,23 @@
         for way in ways:
             remote(*y_copy(way, d - 1, h, False)).wait_recv()
 
-    small[1].wait()
+    def norm(dst, query, inside, carried, scale):
+        for b in range(2):
+            ts = slice(b * tb, (b + 1) * tb)
+            term = dot(query(ts), carried)
+            mixture = inside(ts).astype(F32) + jnp.where(lo_ref[ts, :] < 0, term, 0.0)
+            square_mean = jnp.mean(mixture * mixture, axis=-1, keepdims=True)
+            gains = jnp.broadcast_to(scale[None, :], (tb, DH))
+            dst[ts, :] = (mixture * lax.rsqrt(square_mean + 1e-06) * gains).astype(BF16)
+
     for h in range(heads):
         hs = slice(h * DH, (h + 1) * DH)
         wait_bytes(c_in.at[h, pl.ds(0, sl * (row - 1))], p3r.at[h])
-        carried = c_in[h]
-        scale = jnp.broadcast_to(gain[hs][None, :], (tb, DH))
-        for b in range(2):
-            ts = slice(b * tb, (b + 1) * tb)
-            term = dot(q_ref[ts, hs], carried)
-            mixture = within[h, ts, :] + jnp.where(lo_ref[ts, :] < 0, term, 0.0)
-            square_mean = jnp.mean(mixture * mixture, axis=-1, keepdims=True)
-            norm_all[0, h, ts, :] = (mixture * lax.rsqrt(square_mean + 1e-06) * scale).astype(BF16)
-        y_send(0, h)
+        if h == 0:
+            near_send(3)
+        norm(norm_all.at[0, h], lambda ts: q_ref[ts, hs], lambda ts: within[h, ts, :], c_in[h], gain[hs])
+        if h > 0:
+            y_send(0, h)
 
     def project(rel, start=False):
         for b in range(2):
@@ -271,20 +297,30 @@
             acc[ts, :] = term if start else acc[ts, :] + term
 
     def y_step(d, h):
-        y_wait(d, h)
+        if d == 1 and h == 0:
+            for way in range(2):
+                for kind in range(4):
+                    near_copy(way, kind).wait_recv()
+                norm(
+                    norm_all.at[ny - 1 if way == 0 else 1, 0], lambda ts: q_near[way, ts, :],
+                    lambda ts: in_near[way, ts, :], c_near[way], g_near[way][0:DH])
+        else:
+            y_wait(d, h)
         y_send(d, h)
 
     loads[3].wait()
     project(0, True)
+    wait_bytes(z_block(z, first_rel, yh), wyr)
+    z_step(0, 0)
+    z_step(0, 1)
+    def side(e, core):
+        return e + core * (ny - 2 * e)
+
     y_events = [(d, h) for d in range(1, yh) for h in range(heads)]
     z_events = [(d, half) for d in range(1, zh + 1) for half in range(2)]
-    z_after = [min(2 + m * 3 // 4, len(y_events) - 2) for m in range(len(z_events))]
+    z_after = [min(m + 1, len(y_events) - 2) for m in range(len(z_events))]
     for n, (d, h) in enumerate(y_events):
         y_step(d, h)
-        if n == 0:
-            wait_bytes(z_block(z, first_rel, yh), wyr)
-            z_step(0, 0)
-            z_step(0, 1)
         for after, event in zip(z_after, z_events):
             if after == n:
                 z_step(*event)
@@ -299,16 +335,17 @@
             wait_bytes(z_block(z, first_rel, yh), wys)
         if n == len(y_events) // 2:
             early = len(sends)
+        if n == len(y_events) - 2:
+            for e in range(1, yh - 1):
+                project(side(e, c))
         if n == len(y_events) - 1:
+            project(side(yh - 1, c))
             wait_bytes(wcol.at[pl.ds(twin_rels, yh - 1)], wcr)
             wait_bytes(wcol.at[pl.ds(own_rels, yh - 1)], wcs)
             for copy in sends[:early]:
                 copy.wait_send()
-            for e in range(1, yh - 1):
-                project(e)
-                project(ny - e)
-    project(yh - 1)
-    project(yh + 1)
+            for e in range(1, yh):
+                project(side(e, 1 - c))
     for h in range(heads):
         hs = slice(h * DH, (h + 1) * DH)
         for way in range(2):
@@ -319,6 +356,9 @@
                 acc[ts, :] = total
             else:
                 out_v[ts, :] = total.astype(BF16)
+    for way in range(2):
+        for kind in range(4):
+            near_copy(way, kind).wait_send()
     for copy in sends[early:]:
         copy.wait_send()
 
@@ -351,6 +391,12 @@
             pltpu.VMEM((heads, DH, DH), BF16),
             pltpu.VMEM((tok, DH), jnp.int32),
             pltpu.VMEM((heads, tok, DH), F32),
+            pltpu.VMEM((tok, DH), BF16),
+            pltpu.VMEM((2, tok, DH), BF16),
+            pltpu.VMEM((2, tok, DH), BF16),
+            pltpu.VMEM((2, DH, DH), BF16),
+            pltpu.VMEM((width,), F32),
+            pltpu.VMEM((width,), F32),
             pltpu.VMEM((ny, heads, tok, DH), BF16),
             pltpu.VMEM((ny, width, cols), BF16),
             pltpu.VMEM((tok, cols), F32),
@@ -362,6 +408,7 @@
             dma((2, 2, zh)), dma((2, 2, zh)),
             dma(()), dma(()),
             dma((2, yh, heads)), dma((2, yh, heads)),
+            dma((2, 4)), dma((2, 4)),
         ],
         compiler_params=pltpu.CompilerParams(collective_id=0, has_side_effects=True),
     )(queries, key_vectors, value_vectors, doc_lengths, norm_gain, out_weight)

time: 58.3 us -> 56 us (0.961)
  Pallas kernels: 57.3 us -> 55.1 us
    pallas_call x1, Pallas kernels: 57.3 us -> 55.1 us  [body(): pl.pallas_call(functools.partial(layer_kernel, nz, row, ny), name='layer'...]
where the time goes in v5:
time: 56 us; the launch traced here: 55.9 us
  Pallas kernels  55.1 us (98%)
  local copies, waits for them, and re-layouts  0.8 us (1%)
    pallas_call x1, Pallas kernels, body(): pl.pallas_call(functools.partial(layer_kernel, nz, row, ny), name='layer'...  55.1 us

profile of v5, /device:TPU:1, one launch (start us, length us, event | category | flops | bytes accessed | tf_op | source)
XLA Modules:
  0.0 55.9 jit_solution(8839779915922317201)
XLA Ops:
  0.0 55.1 %layer.1 = bf16[512,512]{1,0:T(8,128)(2,1)S(1)} custom-call(bf16[512,384]{1,0:T(8,128)(2,1)} %q_any.1, bf16[512,384]{1,0:T(8,128)(2,1)} %k_any.1, bf16[512,384]{1,0:T(8,128)(2,1)} %v_any.1, s32[16]{0:T(128)} %lens_any.1, f32[384]{0:T(512)} %gain_any.1, bf16[384,4096]{1,0:T(8,128)(2,1)} %w_any.1), custom_call_target="tpu_custom_call" | custom-call | tf_op jit(solution)/shard_map/layer/pallas_call | solution.py:374
  55.1 0.8 %copy.8 = bf16[512,512]{1,0:T(8,128)(2,1)} copy(bf16[512,512]{1,0:T(8,128)(2,1)S(1)} %layer.1) | data formatting | bytes 1048576

commit v6 on v5

--- a/solution.py
+++ b/solution.py
@@ -22,7 +22,7 @@
     nz, row, ny,
     q_any, k_any, v_any, lens_any, gain_any, w_any, out_v,
     lens, gain, q_ref, k_ref, v_ref, s_loc, s_in, r_in, crow, c_out, c_in, lo_ref, within, within_0, q_near, in_near, c_near, g_below, g_above, norm_all, wcol, acc,
-    load_sem, p1s, p1r, p2s, p2r, p3s, p3r, wys, wyr, wzs, wzr, wcs, wcr, ys, yr, es, er,
+    load_sem, p1s, p1r, p2s, p2r, p3s, p3r, wys, wyr, wzs, wzr, wcs, wcr, ys, yr, es, er, later, level,
 ):
     tok, width = q_ref.shape
     heads = width // DH
@@ -61,10 +61,13 @@
     def far_first(n):
         return sorted(range(1, n), key=lambda k: -min(k, n - k))
 
-    peers = [z_dev((z + k) % nz) for k in far_first(nz)]
-    peers += [y_dev((y + k) % ny) for k in far_first(ny)]
-    peers += [row_dev((r + k) % row) for k in far_first(row)]
+    y_near = (y_dev((y + 1) % ny), y_dev((y + ny - 1) % ny))
+    peers = list(y_near) + [row_dev((r + k) % row) for k in far_first(row)]
     r_in[...] = jnp.zeros_like(r_in)
+    for k in range(nz - 1, 0, -1):
+        @pl.when(z + k < nz)
+        def _():
+            pl.semaphore_signal(barrier, inc=1, device_id=z_dev((z + k) % nz), device_id_type=MESH)
     for peer in peers:
         pl.semaphore_signal(barrier, inc=1, device_id=peer, device_id_type=MESH)
 
@@ -115,7 +118,20 @@
         key = (k_ref[:, hs].astype(F32) * keep).astype(BF16)
         s_loc[h] = dot(key, v_ref[:, hs], ((0,), (0,))).astype(BF16)
 
-    pl.semaphore_wait(barrier, len(peers))
+    pl.semaphore_wait(barrier, len(peers) + z)
+    for k in range(nz - 1, 0, -1):
+        @pl.when(z >= k)
+        def _():
+            pl.semaphore_signal(later, inc=1, device_id=z_dev((z + nz - k) % nz), device_id_type=MESH)
+
+    def relay(n):
+        if n > 0:
+            pl.semaphore_wait(level.at[n - 1], 2)
+        if n < yh - 1:
+            for peer in y_near:
+                pl.semaphore_signal(level.at[n], inc=1, device_id=peer, device_id_type=MESH)
+
+    relay(0)
 
     def part(i):
         return pl.ds(pl.multiple_of(i * sl, 16), sl)
@@ -125,7 +141,6 @@
             i = (r + k) % row
             remote(s_loc.at[h, part(i)], s_in.at[h, r], p1s.at[h], p1r.at[h], row_dev(i)).start()
 
-    y_near = (y_dev((y + 1) % ny), y_dev((y + ny - 1) % ny))
     g_near = (g_below, g_above)
 
     def near_copy(way, kind):
@@ -148,13 +163,6 @@
 
     first_rel = 1 + (yh - 1) * c
     z_rows = pl.ds(pl.multiple_of(z * wr, 16), wr)
-    for i in range(yh):
-        rel = yh + i * (2 * c - 1)
-        plane = (y + ny - rel) % ny
-        remote(
-            w_any.at[z_rows, pl.ds(pl.multiple_of(plane * cols, 128), cols)],
-            wcol.at[rel, z_rows, :], wys, wyr, y_dev(plane)).start()
-
     for h in range(heads):
         s_in[h, r] = s_loc[h, part(r), :]
     lo = jnp.zeros((tok, DH), jnp.int32) - offset
@@ -181,6 +189,7 @@
     within_0[...] = within[0].astype(BF16)
     near_send(2)
 
+    relay(1)
     def p2_copy(h, k, i):
         return remote(
             r_in.at[h, i], r_in.at[h, i], p2s.at[h, k], p2r.at[h, k], z_dev((z + k) % nz))
@@ -191,6 +200,10 @@
         row_sum = functools.reduce(
             jnp.add, [w_row_sum[j] * s_in[h, j].astype(F32) for j in range(row)])
         r_in[h, z] = row_sum.astype(BF16)
+        if h == 0:
+            @pl.when(z < nz - 1)
+            def _():
+                pl.semaphore_wait(later, nz - 1 - z)
         for k in far_first(nz):
             @pl.when(z + k < nz)
             def _():
@@ -207,6 +220,14 @@
             crow[h, i] = total
     attend(1)
 
+    for n in range(2, yh):
+        relay(n)
+    for i in range(yh):
+        rel = yh + i * (2 * c - 1)
+        plane = (y + ny - rel) % ny
+        remote(
+            w_any.at[z_rows, pl.ds(pl.multiple_of(plane * cols, 128), cols)],
+            wcol.at[rel, z_rows, :], wys, wyr, y_dev(plane)).start()
     for h in range(heads):
         for k in range(1, nz):
             @pl.when(z >= k)
@@ -409,6 +430,8 @@
             dma(()), dma(()),
             dma((2, yh, heads)), dma((2, yh, heads)),
             dma((2, 4)), dma((2, 4)),
+            pltpu.SemaphoreType.REGULAR,
+            pltpu.SemaphoreType.REGULAR((yh - 1,)),
         ],
         compiler_params=pltpu.CompilerParams(collective_id=0, has_side_effects=True),
     )(queries, key_vectors, value_vectors, doc_lengths, norm_gain, out_weight)

time: 56 us -> 54.8 us (0.979)
  Pallas kernels: 55.1 us -> 53.7 us
    pallas_call x1, Pallas kernels: 55.1 us -> 53.7 us  [body(): pl.pallas_call(functools.partial(layer_kernel, nz, row, ny), name='layer'...]
where the time goes in v6:
time: 54.8 us; the launch traced here: 54.5 us
  Pallas kernels  53.7 us (98%)
  local copies, waits for them, and re-layouts  0.8 us (1%)
    pallas_call x1, Pallas kernels, body(): pl.pallas_call(functools.partial(layer_kernel, nz, row, ny), name='layer'...  53.7 us

profile of v6, /device:TPU:1, one launch (start us, length us, event | category | flops | bytes accessed | tf_op | source)
XLA Modules:
  0.0 54.5 jit_solution(11514463116620230238)
XLA Ops:
  0.0 53.7 %layer.1 = bf16[512,512]{1,0:T(8,128)(2,1)S(1)} custom-call(bf16[512,384]{1,0:T(8,128)(2,1)} %q_any.1, bf16[512,384]{1,0:T(8,128)(2,1)} %k_any.1, bf16[512,384]{1,0:T(8,128)(2,1)} %v_any.1, s32[16]{0:T(128)} %lens_any.1, f32[384]{0:T(512)} %gain_any.1, bf16[384,4096]{1,0:T(8,128)(2,1)} %w_any.1), custom_call_target="tpu_custom_call" | custom-call | tf_op jit(solution)/shard_map/layer/pallas_call | solution.py:395
  53.7 0.8 %copy.8 = bf16[512,512]{1,0:T(8,128)(2,1)} copy(bf16[512,512]{1,0:T(8,128)(2,1)S(1)} %layer.1) | data formatting | bytes 1048576

commit v7 on v6

--- a/solution.py
+++ b/solution.py
@@ -185,11 +185,12 @@
             scores = jnp.where(allowed, scores, 0.0).astype(BF16)
             within[h, ts, :] = dot(scores, v_ref[:upto, hs])
 
+    relay(1)
     attend(0)
     within_0[...] = within[0].astype(BF16)
     near_send(2)
 
-    relay(1)
+    relay(2)
     def p2_copy(h, k, i):
         return remote(
             r_in.at[h, i], r_in.at[h, i], p2s.at[h, k], p2r.at[h, k], z_dev((z + k) % nz))
@@ -220,7 +221,7 @@
             crow[h, i] = total
     attend(1)
 
-    for n in range(2, yh):
+    for n in range(3, yh):
         relay(n)
     for i in range(yh):
         rel = yh + i * (2 * c - 1)
@@ -339,7 +340,7 @@
 
     y_events = [(d, h) for d in range(1, yh) for h in range(heads)]
     z_events = [(d, half) for d in range(1, zh + 1) for half in range(2)]
-    z_after = [min(m + 1, len(y_events) - 2) for m in range(len(z_events))]
+    z_after = [min(max(m + 1, 2), len(y_events) - 2) for m in range(len(z_events))]
     for n, (d, h) in enumerate(y_events):
         y_step(d, h)
         for after, event in zip(z_after, z_events):

time: 54.8 us -> 55 us (level)
  no operation moved by 1% of the time
where the time goes in v7:
time: 55 us; the launch traced here: 54.9 us
  Pallas kernels  54.1 us (98%)
  local copies, waits for them, and re-layouts  0.8 us (1%)
    pallas_call x1, Pallas kernels, body(): pl.pallas_call(functools.partial(layer_kernel, nz, row, ny), name='layer'...  54.1 us

profile of v7, /device:TPU:1, one launch (start us, length us, event | category | flops | bytes accessed | tf_op | source)
XLA Modules:
  0.0 54.9 jit_solution(11834829687863359422)
XLA Ops:
  0.0 54.1 %layer.1 = bf16[512,512]{1,0:T(8,128)(2,1)S(1)} custom-call(bf16[512,384]{1,0:T(8,128)(2,1)} %q_any.1, bf16[512,384]{1,0:T(8,128)(2,1)} %k_any.1, bf16[512,384]{1,0:T(8,128)(2,1)} %v_any.1, s32[16]{0:T(128)} %lens_any.1, f32[384]{0:T(512)} %gain_any.1, bf16[384,4096]{1,0:T(8,128)(2,1)} %w_any.1), custom_call_target="tpu_custom_call" | custom-call | tf_op jit(solution)/shard_map/layer/pallas_call | solution.py:396
  54.1 0.8 %copy.8 = bf16[512,512]{1,0:T(8,128)(2,1)} copy(bf16[512,512]{1,0:T(8,128)(2,1)S(1)} %layer.1) | data formatting | bytes 1048576
